TPU v7x, 256 devices: a whole 4x4x8 slice. The times are simulated.
256 devices in a mesh: fsdp: 16 (over x, z_lo, core), pair: 16 (over z_hi, y).
Axes of the slice: x: 4, y: 4, z: 8 (z_hi: 4, z_lo: 2; z = z_hi * 2 + z_lo), core: 2. Of those that a mesh axis runs over, the one named last changes fastest.
Arguments:
- tokens: bfloat16 [32768, 8192], P('pair', 'fsdp'), may hold values from -6 to 6
- cotangent: bfloat16 [32768, 1024], P('pair', 'fsdp'), may hold values from -6 to 6
- value_weight: bfloat16 [8192, 1024], P('fsdp'), may hold values from -0.0625 to 0.0625
- adapter_down: bfloat16 [48, 8192, 128], P(None, 'fsdp'), may hold values from -0.0625 to 0.0625
- adapter_up: bfloat16 [48, 128, 1024], P(None, None, 'fsdp'), may hold values from -0.5 to 0.5
- pair_ids: int32 [64], P('pair'), may hold values from 0 to 47
- ranks: int32 [48], replicated, may hold values from 16 to 128, as said below
Outputs:
- input_grad: bfloat16 [32768, 8192], P('pair', 'fsdp')
- down_grad: bfloat16 [48, 8192, 128], P('pair', 'fsdp')
- up_grad: bfloat16 [48, 128, 1024], P('pair', None, 'fsdp')
Inputs may be any that keep to these rules, and one draw needn't show every extreme that they name: `ranks`: each rank is 128, 64, 32 or 16; both ends occur in every draw.
All inputs are finite; a program needn't handle non-finite values.
Results may differ from a plain program's by a relative error of at most 0.022.
Values may be sent and summed in bfloat16 or wider, within the bound.
A program may use at most 128 MiB of HBM per device.

v0:
```python
import math
import jax
import jax.numpy as jnp
from jax import lax
from jax.sharding import PartitionSpec as P


def per_device(tokens, cotangent, value_weight, adapter_down, adapter_up, pair_ids, ranks):
    rows, partial_gradient = tokens.shape
    kvpart = cotangent.shape[1]
    block_count = pair_ids.shape[0]
    block_length = rows // block_count
    npair, _, rmax = adapter_down.shape
    norm = 1.0 / math.sqrt(rows * lax.axis_size("pair"))
    columns = jnp.arange(rmax, dtype=jnp.int32)
    mask = (columns[None, :] < ranks[:, None]).astype(jnp.float32)
    scale = 32.0 / ranks.astype(jnp.float32)
    x_blocks = tokens.reshape(block_count, block_length, partial_gradient)
    c_blocks = cotangent.reshape(block_count, block_length, kvpart)
    selected_down_adapter = adapter_down[pair_ids]
    b_sel = adapter_up[pair_ids]
    low_part = jnp.einsum(
        "btd,bdr->btr", x_blocks, selected_down_adapter, preferred_element_type=jnp.float32
    )
    back_part = jnp.einsum("btk,brk->btr", c_blocks, b_sel, preferred_element_type=jnp.float32)
    low_full, back_full = (
        lax.psum(low_part.astype(jnp.bfloat16), "fsdp").astype(jnp.float32),
        lax.psum(back_part.astype(jnp.bfloat16), "fsdp").astype(jnp.float32),
    )
    rows_mask = mask[pair_ids][:, None, :]
    low_b = (low_full * rows_mask).astype(jnp.bfloat16)
    backward_up_part = (back_full * rows_mask).astype(jnp.bfloat16)
    whole_weight = lax.all_gather(value_weight, "fsdp", axis=0, tiled=True)
    cot_rows = lax.all_to_all(cotangent, "fsdp", split_axis=0, concat_axis=1, tiled=True)
    product = jnp.einsum(
        "tk,dk->td", cot_rows, whole_weight, preferred_element_type=jnp.float32
    ).astype(jnp.bfloat16)
    frozen_output = lax.all_to_all(product, "fsdp", split_axis=1, concat_axis=0, tiled=True)
    block_offset = scale[pair_ids]
    adapter_output = jnp.einsum(
        "eiz,efz->eif", backward_up_part, selected_down_adapter, preferred_element_type=jnp.float32
    )
    input_grad = (
        frozen_output.reshape(block_count, block_length, partial_gradient).astype(jnp.float32)
        + block_offset[:, None, None] * adapter_output
    ).astype(jnp.bfloat16)
    coef = block_offset * norm
    term_a = (
        jnp.einsum("btd,btr->bdr", x_blocks, backward_up_part, preferred_element_type=jnp.float32)
        * coef[:, None, None]
    )
    term_b = (
        jnp.einsum("btr,btk->brk", low_b, c_blocks, preferred_element_type=jnp.float32)
        * coef[:, None, None]
    )
    onehot = (pair_ids[:, None] == jnp.arange(npair, dtype=jnp.int32)[None, :]).astype(jnp.float32)
    part_a = jnp.einsum("bp,bdr->pdr", onehot, term_a)
    part_b = jnp.einsum("bp,brk->prk", onehot, term_b)
    down_grad, up_grad = (
        lax.psum_scatter(
            part_a.astype(jnp.bfloat16), "pair", scatter_dimension=0, tiled=True
        ).astype(jnp.float32),
        lax.psum_scatter(
            part_b.astype(jnp.bfloat16), "pair", scatter_dimension=0, tiled=True
        ).astype(jnp.float32),
    )
    return (
        input_grad.reshape(rows, partial_gradient),
        down_grad.astype(jnp.bfloat16),
        up_grad.astype(jnp.bfloat16),
    )


def solution(mesh):
    placed = (
        P("pair", "fsdp"),
        P("pair", "fsdp"),
        P("fsdp", None),
        P(None, "fsdp", None),
        P(None, None, "fsdp"),
        P("pair"),
        P(),
    )
    return jax.shard_map(
        per_device,
        mesh=mesh,
        in_specs=placed,
        out_specs=(P("pair", "fsdp"), P("pair", "fsdp", None), P("pair", None, "fsdp")),
        check_vma=False,
    )
```

profile of v0, /device:TPU:1, one launch (start us, length us, event | category | flops | bytes accessed | tf_op | source)
XLA Modules:
  0.0 455.5 jit_solution(17975335476844694819)
XLA Ops:
  7.2 0.8 compare_select_fusion
  8.1 3.4 gather_fusion.3
  11.5 1.7 gather_fusion.1
  13.2 2.1 fusion.1
  15.3 1.6 fusion.2
  17.0 0.7 all-gather.2.cloned.1.call-update
  17.8 0.6 gather_fusion
  18.5 0.6 gather_fusion.2
  19.1 126.9 %all-reduce.3.cloned.1.call-done = (bf16[4,512,128]{1,2,0:T(8,128)(2,1)}, bf16[4,512,128]{1,2,0:T(8,128)(2,1)}) async-done(((bf16[4,512,128]{1,2,0:T(8,128)(2,1)}, bf16[4,512,128]{1,2,0:T(8,128)(2,1)}), (bf16[4,512,128]{1,2,0:T(8,128)(2,1)}, bf16[4,512,128]{1,2,0:T(8,128)(2,1)})) %all-reduce.3.cloned.1.call-update) | async-done | bytes 1048592 | tf_op jit(solution)/shard_map/psum | solution.py:28
  145.9 1.4 convolution_multiply_fusion.1
  147.9 1.1 copy.41
  149.1 1.5 fusion
  150.6 1.1 copy.35
  151.7 3.0 convolution_convert_fusion.1
  154.7 4.3 copy.36
  159.0 16.1 %all_to_all.32 = bf16[16,128,64]{1,2,0:T(8,128)(2,1)S(1)} all-to-all(bf16[16,128,64]{1,2,0:T(8,128)(2,1)S(1)} %copy_bitcast_fusion.1), channel_id=1, replica_groups=mesh['fsdp'=16,'pair'=16] {'fsdp'}, dimensions={0} | all-to-all | bytes 524288 | tf_op jit(solution)/shard_map/all_to_all | solution.py:34
  175.2 70.6 %all-gather.2.cloned.1.call-done = bf16[8192,1024]{1,0:T(8,128)(2,1)} async-done(((bf16[512,1024]{1,0:T(8,128)(2,1)}), bf16[8192,1024]{1,0:T(8,128)(2,1)}) %all-gather.2.cloned.1.call-update) | async-done | bytes 16777232 | tf_op jit(solution)/shard_map/all_gather | solution.py:33
  245.8 12.8 %convolution_convert_fusion = bf16[128,8192]{1,0:T(8,128)(2,1)} fusion(bf16[128,1024]{0,1:T(8,128)(2,1)S(1)} %bitcast.47, bf16[8192,1024]{1,0:T(8,128)(2,1)} %all-gather.2.cloned.1.call-done), kind=kOutput, calls=%fused_computation.4 | convolution fusion | flops 2148532224 | bytes 19136512 | tf_op jit(solution)/shard_map/tk,dk->td/dot_general | solution.py:35
  258.5 1.8 copy.60
  260.3 35.4 %all_to_all.33 = bf16[128,16,512]{2,0,1:T(8,128)(2,1)S(1)} all-to-all(bf16[128,16,512]{2,0,1:T(8,128)(2,1)S(1)} %bitcast.44), channel_id=1, replica_groups=mesh['fsdp'=16,'pair'=16] {'fsdp'}, dimensions={1} | all-to-all | bytes 4194304 | tf_op jit(solution)/shard_map/all_to_all | solution.py:38
  295.8 0.6 convert_element_type.74
  296.8 2.4 add_convert_fusion
  299.2 36.5 %reduce-scatter.5.cloned.1.call-done = bf16[3,128,64]{1,2,0:T(8,128)(2,1)} async-done(((bf16[48,128,64]{1,2,0:T(8,128)(2,1)}), bf16[3,128,64]{1,2,0:T(8,128)(2,1)}) %reduce-scatter.5.cloned.1.call-update) | async-done | bytes 49168 | tf_op jit(solution)/shard_map/reduce_scatter | solution.py:63
  335.7 113.2 %reduce-scatter.3.cloned.1.call-done = bf16[3,512,128]{2,1,0:T(8,128)(2,1)} async-done(((bf16[48,512,128]{2,1,0:T(8,128)(2,1)}), bf16[3,512,128]{2,1,0:T(8,128)(2,1)}) %reduce-scatter.3.cloned.1.call-update) | async-done | bytes 393232 | tf_op jit(solution)/shard_map/reduce_scatter | solution.py:60
  (23 shorter events, 1.4 us)
Async XLA Ops:
  7.2 8.1 %copy-start = (bf16[2048,512]{1,0:T(8,128)(2,1)S(1)}, bf16[2048,512]{1,0:T(8,128)(2,1)}, u32[]{:S(2)}) copy-start(bf16[2048,512]{1,0:T(8,128)(2,1)} %param.7) | copy-start | bytes 6291460
  7.2 138.8 %copy-start.2 = (bf16[2048,64]{0,1:T(8,128)(2,1)S(1)}, bf16[2048,64]{0,1:T(8,128)(2,1)}, u32[]{:S(2)}) copy-start(bf16[2048,64]{0,1:T(8,128)(2,1)} %param.8) | copy-start | bytes 786436
  7.2 10.6 %copy-start.4 = (s32[48]{0:T(128)S(1)}, s32[48]{0:T(128)}, u32[]{:S(2)}) copy-start(s32[48]{0:T(128)} %param.13) | copy-start | bytes 580
  7.2 138.7 %all-reduce.3.cloned.1.call-start = ((), (), s32[]{:S(2)}) async-start(), calls=%async_computation.7 | async-start | bytes 2097152 | tf_op jit(solution)/shard_map/psum | solution.py:28
  11.5 135.9 %copy-start.3 = (s32[4]{0:T(128)S(1)}, s32[4]{0:T(128)}, u32[]{:S(2)}) copy-start(s32[4]{0:T(128)} %param.12) | copy-start | bytes 52
  16.9 228.8 %all-gather.2.cloned.1.call-start = ((), (), s32[]{:S(2)}) async-start(), calls=%async_computation.4 | async-start | bytes 17825792 | tf_op jit(solution)/shard_map/all_gather | solution.py:33
  17.7 318.0 %reduce-scatter.5.cloned.1.call-start = ((), (), s32[]{:S(2)}) async-start(), calls=%async_computation.6 | async-start | bytes 835584 | tf_op jit(solution)/shard_map/reduce_scatter | solution.py:63
  149.0 299.9 %reduce-scatter.3.cloned.1.call-start = ((), (), s32[]{:S(2)}) async-start(), calls=%async_computation.5 | async-start | bytes 6684672 | tf_op jit(solution)/shard_map/reduce_scatter | solution.py:60
  295.8 1.0 copy-start.1
Sparse Core Ops, SparseCore 0:
  17.1 128.8 all-reduce.2
  147.8 97.9 all-gather.1
  249.8 85.8 reduce-scatter.4
  339.9 109.0 reduce-scatter.2
where the time goes:
time: 456 us; the launch traced here: 455 us
  waiting for transfers between devices  348 us (76%)
  blocking collectives  51.6 us (11%)
  matrix products  25.3 us (6%)
  local copies, waits for them, and re-layouts  15.2 us (3%)
  between operations  13.9 us (3%)
    psum x1, waiting for transfers between devices, per_device(): lax.psum(back_part.astype(jnp.bfloat16), 'fsdp').astype(jnp.float32)  127 us
    reduce_scatter x1, waiting for transfers between devices, per_device(): lax.psum_scatter(part_a.astype(jnp.bfloat16), 'pair', scatter_dimension=0...  113 us
    all_gather x1, waiting for transfers between devices, per_device(): whole_weight = lax.all_gather(value_weight, 'fsdp', axis=0, tiled=True)  70.6 us
    reduce_scatter x1, waiting for transfers between devices, per_device(): lax.psum_scatter(part_b.astype(jnp.bfloat16), 'pair', scatter_dimension=0...  36.5 us
    all_to_all x1, blocking collectives, per_device(): lax.all_to_all(product, 'fsdp', split_axis=1, concat_axis=0, tiled=True)  35.4 us
    all_to_all x1, blocking collectives, per_device(): lax.all_to_all(cotangent, 'fsdp', split_axis=0, concat_axis=1, tiled=True)  16.1 us
    dot_general x1, matrix products, per_device(): jnp.einsum('tk,dk->td', cot_rows, whole_weight, preferred_element_type=jn...  12.8 us
  transfers between devices with their start and end apart: 4, of which 4 were waited for; matrix products, arithmetic and copies ran while one was open for 7% of the time, Pallas kernels for 0%

commit v1 on v0

--- a/solution.py
+++ b/solution.py
@@ -30,7 +30,9 @@
     rows_mask = mask[pair_ids][:, None, :]
     low_b = (low_full * rows_mask).astype(jnp.bfloat16)
     backward_up_part = (back_full * rows_mask).astype(jnp.bfloat16)
-    whole_weight = lax.all_gather(value_weight, "fsdp", axis=0, tiled=True)
+    whole_weight = jnp.concatenate(
+        lax.all_to_all(jnp.stack([value_weight] * lax.axis_size("fsdp")), "fsdp", 0, 0), axis=0
+    )
     cot_rows = lax.all_to_all(cotangent, "fsdp", split_axis=0, concat_axis=1, tiled=True)
     product = jnp.einsum(
         "tk,dk->td", cot_rows, whole_weight, preferred_element_type=jnp.float32

time: 456 us -> 394 us (0.86)
  waiting for transfers between devices: 348 us -> 276 us
  local copies, waits for them, and re-layouts: 15.2 us -> 22.4 us
  starting transfers between devices: 0.16 us -> 6.05 us
    all_gather x1 -> x0, waiting for transfers between devices: 70.6 us -> none  [per_device(): whole_weight = lax.all_gather(value_weight, 'fsdp', axis=0, tiled=True)]
    all_to_all x0 -> x1, waiting for transfers between devices: none -> 54.9 us  [per_device(): lax.all_to_all(jnp.stack([value_weight] * lax.axis_size('fsdp')), 'fsdp',...]
    reduce_scatter x1, waiting for transfers between devices: 36.5 us -> 0.01 us  [per_device(): lax.psum_scatter(part_b.astype(jnp.bfloat16), 'pair', scatter_dimension=0...]
    reduce_scatter x1, waiting for transfers between devices: 113 us -> 85.3 us  [per_device(): lax.psum_scatter(part_a.astype(jnp.bfloat16), 'pair', scatter_dimension=0...]
    psum x1, waiting for transfers between devices: 127 us -> 136 us  [per_device(): lax.psum(back_part.astype(jnp.bfloat16), 'fsdp').astype(jnp.float32)]
    another operation x0 -> x1, local copies, waits for them, and re-layouts: none -> 6.9 us  [per_device(): jnp.stack([value_weight] * lax.axis_size('fsdp'))]
    all_to_all x0 -> x1, starting transfers between devices: none -> 5.92 us  [per_device(): lax.all_to_all(jnp.stack([value_weight] * lax.axis_size('fsdp')), 'fsdp',...]
  transfers between devices with their start and end apart: 4 -> 4, of which waited for: 4 -> 3; matrix products, arithmetic and copies ran while one was open for 7% -> 10% of each run, Pallas kernels for 0% -> 0%
where the time goes in v1:
time: 394 us; the launch traced here: 393 us
  waiting for transfers between devices  276 us (70%)
  blocking collectives  50.3 us (13%)
  matrix products  23.4 us (6%)
  local copies, waits for them, and re-layouts  22.4 us (6%)
  between operations  13.9 us (4%)
  starting transfers between devices  6.05 us (2%)
    psum x1, waiting for transfers between devices, per_device(): lax.psum(back_part.astype(jnp.bfloat16), 'fsdp').astype(jnp.float32)  136 us
    reduce_scatter x1, waiting for transfers between devices, per_device(): lax.psum_scatter(part_a.astype(jnp.bfloat16), 'pair', scatter_dimension=0...  85.3 us
    all_to_all x1, waiting for transfers between devices, per_device(): lax.all_to_all(jnp.stack([value_weight] * lax.axis_size('fsdp')), 'fsdp',...  54.9 us
    all_to_all x1, blocking collectives, per_device(): lax.all_to_all(product, 'fsdp', split_axis=1, concat_axis=0, tiled=True)  36.2 us
    all_to_all x1, blocking collectives, per_device(): lax.all_to_all(cotangent, 'fsdp', split_axis=0, concat_axis=1, tiled=True)  14.1 us
    dot_general x1, matrix products, per_device(): jnp.einsum('tk,dk->td', cot_rows, whole_weight, preferred_element_type=jn...  12.7 us
  transfers between devices with their start and end apart: 4, of which 3 were waited for; matrix products, arithmetic and copies ran while one was open for 10% of the time, Pallas kernels for 0%

profile of v1, /device:TPU:1, one launch (start us, length us, event | category | flops | bytes accessed | tf_op | source)
XLA Modules:
  0.0 393.0 jit_solution(2652157736776624010)
XLA Ops:
  7.2 1.2 copy_bitcast_fusion.1
  8.3 14.1 %all_to_all.37 = bf16[16,128,64]{1,2,0:T(8,128)(2,1)S(1)} all-to-all(bf16[16,128,64]{1,2,0:T(8,128)(2,1)S(1)} %copy_bitcast_fusion.1), channel_id=1, replica_groups=mesh['fsdp'=16,'pair'=16] {'fsdp'}, dimensions={0} | all-to-all | bytes 524288 | tf_op jit(solution)/shard_map/all_to_all | solution.py:36
  22.5 6.9 %stack.2 = bf16[16,512,1024]{2,1,0:T(8,128)(2,1)} broadcast(bf16[512,1024]{1,0:T(8,128)(2,1)} %param.9), dimensions={1,2} | broadcast | bytes 17825792 | tf_op jit(solution)/shard_map/stack | solution.py:34
  29.4 5.9 %all-to-all-start.1 = ((bf16[16,512,1024]{2,1,0:T(8,128)(2,1)}), bf16[16,512,1024]{2,1,0:T(8,128)(2,1)}, u32[]{:S(2)}, u32[]{:S(2)}) async-start(bf16[16,512,1024]{2,1,0:T(8,128)(2,1)} %stack.2), calls=%async_computation.1 | async-start | bytes 33554432 | tf_op jit(solution)/shard_map/all_to_all | solution.py:34
  35.4 3.4 gather_fusion.3
  38.9 1.7 gather_fusion.1
  40.6 1.1 fusion.1
  41.7 1.7 fusion.2
  43.5 0.6 gather_fusion
  44.2 0.6 gather_fusion.2
  44.7 136.0 %all-reduce.3.cloned.1.call-done = (bf16[4,512,128]{1,2,0:T(8,128)(2,1)}, bf16[4,512,128]{1,2,0:T(8,128)(2,1)}) async-done(((bf16[4,512,128]{1,2,0:T(8,128)(2,1)}, bf16[4,512,128]{1,2,0:T(8,128)(2,1)}), (bf16[4,512,128]{1,2,0:T(8,128)(2,1)}, bf16[4,512,128]{1,2,0:T(8,128)(2,1)})) %all-reduce.3.cloned.1.call-update) | async-done | bytes 1048592 | tf_op jit(solution)/shard_map/psum | solution.py:28
  180.7 1.4 convolution_multiply_fusion.1
  182.2 0.5 convolution_convert_fusion.2
  182.7 1.1 copy.41
  183.9 1.5 fusion
  185.8 1.9 convolution_convert_fusion.1
  187.7 4.2 %copy.36 = bf16[48,512,128]{2,1,0:T(8,128)(2,1)} copy(bf16[48,512,128]{2,0,1:T(8,128)(2,1)S(1)} %convolution_convert_fusion.1) | data formatting | bytes 12582912 | tf_op jit(solution)/shard_map/convert_element_type | solution.py:63
  191.9 54.9 %all-to-all-done.1 = bf16[16,512,1024]{2,1,0:T(8,128)(2,1)} async-done(((bf16[16,512,1024]{2,1,0:T(8,128)(2,1)}), bf16[16,512,1024]{2,1,0:T(8,128)(2,1)}, u32[]{:S(2)}, u32[]{:S(2)}) %all-to-all-start.1) | async-done | bytes 16777248 | tf_op jit(solution)/shard_map/all_to_all | solution.py:34
  246.9 12.7 %convolution_convert_fusion = bf16[128,8192]{1,0:T(8,128)(2,1)} fusion(bf16[128,1024]{0,1:T(8,128)(2,1)S(1)} %bitcast.48, bf16[8192,1024]{1,0:T(8,128)(2,1)} %bitcast.2), kind=kOutput, calls=%fused_computation.4 | convolution fusion | flops 2148532224 | bytes 19136512 | tf_op jit(solution)/shard_map/tk,dk->td/dot_general | solution.py:37
  259.6 1.8 copy.60
  261.4 36.2 %all_to_all.38 = bf16[128,16,512]{2,0,1:T(8,128)(2,1)S(1)} all-to-all(bf16[128,16,512]{2,0,1:T(8,128)(2,1)S(1)} %bitcast.45), channel_id=1, replica_groups=mesh['fsdp'=16,'pair'=16] {'fsdp'}, dimensions={1} | all-to-all | bytes 4194304 | tf_op jit(solution)/shard_map/all_to_all | solution.py:40
  297.6 0.6 convert_element_type.74
  298.7 2.4 add_convert_fusion
  301.1 85.3 %reduce-scatter.3.cloned.1.call-done = bf16[3,512,128]{2,1,0:T(8,128)(2,1)} async-done(((bf16[48,512,128]{2,1,0:T(8,128)(2,1)}), bf16[3,512,128]{2,1,0:T(8,128)(2,1)}) %reduce-scatter.3.cloned.1.call-update) | async-done | bytes 393232 | tf_op jit(solution)/shard_map/reduce_scatter | solution.py:62
  (25 shorter events, 1.1 us)
Async XLA Ops:
  7.2 34.5 %copy-start = (bf16[2048,512]{1,0:T(8,128)(2,1)S(1)}, bf16[2048,512]{1,0:T(8,128)(2,1)}, u32[]{:S(2)}) copy-start(bf16[2048,512]{1,0:T(8,128)(2,1)} %param.7) | copy-start | bytes 6291460
  29.4 6.0 %copy-start.4 = (s32[4]{0:T(128)S(1)}, s32[4]{0:T(128)}, u32[]{:S(2)}) copy-start(s32[4]{0:T(128)} %param.12) | copy-start | bytes 52
  29.4 11.2 %copy-start.3 = (bf16[2048,64]{0,1:T(8,128)(2,1)S(1)}, bf16[2048,64]{0,1:T(8,128)(2,1)}, u32[]{:S(2)}) copy-start(bf16[2048,64]{0,1:T(8,128)(2,1)} %param.8) | copy-start | bytes 786436
  29.4 217.5 %all-to-all-start.1 = ((bf16[16,512,1024]{2,1,0:T(8,128)(2,1)}), bf16[16,512,1024]{2,1,0:T(8,128)(2,1)}, u32[]{:S(2)}, u32[]{:S(2)}) async-start(bf16[16,512,1024]{2,1,0:T(8,128)(2,1)} %stack.2), calls=%async_computation.1 | async-start | bytes 33554432 | tf_op jit(solution)/shard_map/all_to_all | solution.py:34
  35.3 8.1 %copy-start.5 = (s32[48]{0:T(128)S(1)}, s32[48]{0:T(128)}, u32[]{:S(2)}) copy-start(s32[48]{0:T(128)} %param.13) | copy-start | bytes 580
  35.3 145.4 %all-reduce.3.cloned.1.call-start = ((), (), s32[]{:S(2)}) async-start(), calls=%async_computation.7 | async-start | bytes 2097152 | tf_op jit(solution)/shard_map/psum | solution.py:28
  43.4 257.8 %reduce-scatter.5.cloned.1.call-start = ((), (), s32[]{:S(2)}) async-start(), calls=%async_computation.6 | async-start | bytes 835584 | tf_op jit(solution)/shard_map/reduce_scatter | solution.py:65
  183.9 202.6 %reduce-scatter.3.cloned.1.call-start = ((), (), s32[]{:S(2)}) async-start(), calls=%async_computation.5 | async-start | bytes 6684672 | tf_op jit(solution)/shard_map/reduce_scatter | solution.py:62
  297.6 1.1 copy-start.2
  297.6 88.8 %copy-start.1 = (bf16[2048,512]{1,0:T(8,128)(2,1)S(1)}, bf16[2048,512]{1,0:T(8,128)(2,1)}, u32[]{:S(2)}) copy-start(bf16[2048,512]{1,0:T(8,128)(2,1)} %param.7) | copy-start | bytes 6291460
Sparse Core Ops, SparseCore 0:
  43.5 137.1 all-reduce.2
  184.8 86.6 reduce-scatter.4
  275.8 110.5 reduce-scatter.2
